TPU v7x, 32 devices: a whole 2x2x4 slice. The times are simulated.
32 devices in a mesh: seq: 8 (over z, x), doc: 4 (over y, core).
Axes of the slice: x: 2, y: 2, z: 4, core: 2. Of those that a mesh axis runs over, the one named last changes fastest.
Arguments:
- tokens: bfloat16 [16, 8192, 512], P('doc', 'seq'), may hold values from -6 to 6
- factor_one: bfloat16 [8, 1024, 1024], P('seq'), may hold values from -0.1875 to 0.1875
- factor_two: bfloat16 [1024, 8, 8], P('seq'), may hold values from -2 to 2
- gate_gain: float32 [512], replicated, may hold values from 0.5 to 2
- gate_bias: float32 [512], replicated, may hold values from -4 to 4
- block_counts: int32 [16], replicated, may hold values from 7 to 8, as said below
- partner: int32 [16], replicated, may hold values from 0 to 15, as said below
- reading: float32 [512, 256], replicated, may hold values from -0.25 to 0.25
Outputs:
- gated: bfloat16 [16, 8, 1024, 512], P('doc', None, 'seq')
- contrast: float32 [16, 256], P('doc')
Inputs may be any that keep to these rules, and one draw needn't show every extreme that they name: `block_counts`: some document has all 8 blocks valid and another exactly 7. partner is a single cycle through all documents; no document is its own partner.
All inputs are finite; a program needn't handle non-finite values.
Results may differ from a plain program's by a relative error of at most 0.005.
Values may be sent and summed in bfloat16 or wider, within the bound.
A program may use at most 128 MiB of HBM per device.

v0:
```python
import jax
import jax.numpy as jnp
from jax import lax
from jax.sharding import PartitionSpec as P


def shards(tokens, factor_one, factor_two, gate_gain, gate_bias, block_counts, partner, reading):
    doc_dev, tok_dev, chan = tokens.shape
    blocks_dev, blk_size = (factor_one.shape[0], factor_one.shape[1])
    all_blocks = factor_two.shape[1]
    all_docs = block_counts.shape[0]
    doc_start = lax.axis_index("doc") * doc_dev
    block_start = lax.axis_index("seq") * blocks_dev
    local_counts = lax.dynamic_slice_in_dim(block_counts, doc_start, doc_dev)
    block_ids = block_start + jnp.arange(blocks_dev, dtype=jnp.int32)
    inside = (block_ids[None, :] < local_counts[:, None]).astype(jnp.bfloat16)
    grid = tokens.reshape(doc_dev, blocks_dev, blk_size, chan) * inside[:, :, None, None]
    mixed = jnp.einsum(
        "dbic,bij->dbjc", grid, factor_one, preferred_element_type=jnp.float32
    ).astype(jnp.bfloat16)
    values_t, inputs_t = (
        lax.all_to_all(mixed, "seq", split_axis=2, concat_axis=1, tiled=True),
        lax.all_to_all(grid, "seq", split_axis=2, concat_axis=1, tiled=True),
    )
    second = jnp.einsum("dpjc,jpq->dqjc", values_t, factor_two, preferred_element_type=jnp.float32)
    gate = jax.nn.sigmoid(gate_gain * inputs_t.astype(jnp.float32) + gate_bias)
    full = second * gate
    gated = full.astype(jnp.bfloat16)
    row_ids = jnp.arange(all_blocks, dtype=jnp.int32)
    keep = (row_ids[None, :] < local_counts[:, None]).astype(jnp.float32)
    partial_value = jnp.sum(full * keep[:, :, None, None], axis=(1, 2))
    scale_local = 1.0 / jnp.sqrt(local_counts.astype(jnp.float32) * blk_size)
    mine = lax.psum(partial_value, "seq") * scale_local[:, None]
    pooled_all = lax.all_gather(mine, "doc", axis=0, tiled=True)
    local_partner = lax.dynamic_slice_in_dim(partner, doc_start, doc_dev)
    picker = (local_partner[:, None] == jnp.arange(all_docs, dtype=jnp.int32)[None, :]).astype(
        jnp.float32
    )
    other = jnp.dot(picker, pooled_all, precision=lax.Precision.HIGHEST)
    contrast = jnp.dot(mine - other, reading, precision=lax.Precision.HIGHEST)
    return (gated, contrast)


def solution(mesh):
    placed = (
        P("doc", "seq", None),
        P("seq", None, None),
        P("seq", None, None),
        P(),
        P(),
        P(),
        P(),
        P(),
    )
    return jax.shard_map(
        shards,
        mesh=mesh,
        in_specs=placed,
        out_specs=(P("doc", None, "seq", None), P("doc", None)),
        check_vma=False,
    )
```

profile of v0, /device:TPU:0, one launch (start us, length us, event | category | flops | bytes accessed | tf_op | source)
XLA Modules:
  0.0 254.0 jit_solution(281498161123050045)
XLA Ops:
  0.6 0.0 copy-start
  0.7 0.9 multiply_rsqrt_fusion
  1.5 7.5 %fusion.21 = bf16[4,1,1024,512]{3,0,1,2:T(4,128)(2,1)} fusion(bf16[4]{0:T(256)(128)(2,1)S(1)} %compare_convert_fusion, bf16[4,1024,512]{2,1,0:T(8,128)(2,1)} %param.8), kind=kLoop, calls=%fused_computation.24 | loop fusion | flops 2097152 | bytes 8388616 | tf_op jit(solution)/shard_map/mul | solution.py:17
  9.0 7.3 %all-to-all-start.1 = ((bf16[4,1,1024,512]{3,0,1,2:T(4,128)(2,1)}), bf16[4,1,1024,512]{3,0,1,2:T(4,128)(2,1)}, u32[]{:S(2)}, u32[]{:S(2)}) async-start(bf16[4,1,1024,512]{3,0,1,2:T(4,128)(2,1)} %fusion.21), calls=%async_computation.1 | async-start | bytes 8388608 | tf_op jit(solution)/shard_map/all_to_all | solution.py:23
  16.2 5.4 %copy_multiply_fusion.1 = bf16[4,1024,512]{2,0,1:T(4,128)(2,1)S(1)} fusion(bf16[4,1024,512]{2,1,0:T(8,128)(2,1)} %param.8, bf16[4]{0:T(256)(128)(2,1)S(1)} %compare_convert_fusion), kind=kLoop, calls=%fused_computation.12 | loop fusion | flops 2097152 | bytes 8388616 | tf_op jit(solution)/shard_map/mul | solution.py:17
  21.7 0.0 copy-done
  21.7 6.5 %convert_bitcast_fusion = bf16[4,1,1024,512]{2,3,0,1:T(8,128)(2,1)} fusion(bf16[4,1024,512]{2,0,1:T(4,128)(2,1)S(1)} %copy_multiply_fusion.1, bf16[1,1024,1024]{2,1,0:T(8,128)(2,1)S(1)} %copy-done), kind=kOutput, calls=%fused_computation.13 | convolution fusion | flops 4297064448 | bytes 10485760 | tf_op jit(solution)/shard_map/dbic,bij->dbjc/dot_general | solution.py:18
  28.2 7.9 %copy.28 = bf16[4,1,1024,512]{3,0,1,2:T(4,128)(2,1)} copy(bf16[4,1,1024,512]{2,3,0,1:T(8,128)(2,1)} %convert_bitcast_fusion) | data formatting | bytes 8388608 | tf_op jit(solution)/shard_map/convert_element_type | solution.py:20
  36.0 0.0 copy-start.5
  36.0 0.0 copy-start.2
  36.0 73.5 %all-to-all-done.1 = bf16[4,1,1024,512]{3,0,1,2:T(4,128)(2,1)} async-done(((bf16[4,1,1024,512]{3,0,1,2:T(4,128)(2,1)}), bf16[4,1,1024,512]{3,0,1,2:T(4,128)(2,1)}, u32[]{:S(2)}, u32[]{:S(2)}) %all-to-all-start.1) | async-done | bytes 4194336 | tf_op jit(solution)/shard_map/all_to_all | solution.py:23
  109.5 4.8 %all-to-all-start = ((bf16[4,1,1024,512]{3,0,1,2:T(4,128)(2,1)}), bf16[4,1,1024,512]{3,0,1,2:T(4,128)(2,1)}, u32[]{:S(2)}, u32[]{:S(2)}) async-start(bf16[4,1,1024,512]{3,0,1,2:T(4,128)(2,1)} %copy.28), calls=%async_computation | async-start | bytes 8388608 | tf_op jit(solution)/shard_map/all_to_all | solution.py:22
  114.3 0.0 copy-done.5
  114.3 0.1 dynamic_slice.7
  114.4 0.0 copy-done.2
  114.4 0.2 copy.35
  114.6 0.1 fusion.14
  114.7 3.0 %copy.32 = bf16[4,1,1024,512]{3,2,0,1:T(8,128)(2,1)S(1)} copy(bf16[4,1,1024,512]{3,0,1,2:T(4,128)(2,1)} %all-to-all-done.1) | data formatting | bytes 8388608 | tf_op jit(solution)/shard_map/all_to_all | solution.py:23
  117.7 0.0 copy-start.3
  117.7 0.0 copy-start.4
  117.7 4.4 %convert.1 = f32[4,8,128,512]{3,2,1,0:T(8,128)} convert(bf16[4,8,128,512]{3,2,1,0:T(8,128)(2,1)S(1)} %bitcast.24) | non-fusion elementwise | flops 2097152 | bytes 12582912 | tf_op jit(solution)/shard_map/convert_element_type | solution.py:26
  122.1 84.6 %all-to-all-done = bf16[4,1,1024,512]{3,0,1,2:T(4,128)(2,1)} async-done(((bf16[4,1,1024,512]{3,0,1,2:T(4,128)(2,1)}), bf16[4,1,1024,512]{3,0,1,2:T(4,128)(2,1)}, u32[]{:S(2)}, u32[]{:S(2)}) %all-to-all-start) | async-done | bytes 4194336 | tf_op jit(solution)/shard_map/all_to_all | solution.py:22
  206.7 0.0 copy-done.3
  206.7 0.0 copy-done.4
  206.7 14.7 %multiply_reduce_fusion = (f32[4,512]{1,0:T(4,128)S(1)}, bf16[4,8,128,512]{3,1,0,2:T(8,128)(2,1)}) fusion(f32[4,8]{1,0:T(4,128)S(1)} %fusion.14, f32[512]{0:T(512)S(1)} %copy-done.3, f32[4,8,128,512]{3,2,1,0:T(8,128)} %convert.1, f32[512]{0:T(512)S(1)} %copy-done.4, bf16[128,8,8,1]{1,2,3,0:T(8,128)(2,1)S(1)} %copy.35, bf16[4,8,128,512]{3,0,2,1:T(4,128)(2,1)} %bitcast.5), kind=kOutput, calls=%fused_computation.7 | convolution fusion | flops 52426752 | bytes 16806016 | tf_op jit(solution)/shard_map/dpjc,jpq->dqjc/dot_general | solution.py:25
  221.4 19.6 %psum.7 = f32[4,512]{1,0:T(4,128)S(1)} all-reduce(f32[4,512]{1,0:T(4,128)S(1)} %get-tuple-element.12), channel_id=1, replica_groups=mesh['seq'=8,'doc'=4] {'seq'}, use_global_device_ids=true, to_apply=%region_1.0 | all-reduce | flops 2048 | bytes 16384 | tf_op jit(solution)/shard_map/psum | solution.py:33
  241.0 0.1 multiply_bitcast_fusion
  241.1 5.2 %all-gather = f32[4,4,512]{2,1,0:T(4,128)S(1)} all-gather(f32[1,4,512]{2,1,0:T(4,128)S(1)} %multiply_bitcast_fusion), channel_id=1, replica_groups=mesh['seq'=8,'doc'=4] {'doc'}, dimensions={0}, use_global_device_ids=true | all-gather | bytes 40960 | tf_op jit(solution)/shard_map/all_gather | solution.py:34
  246.3 0.0 copy-start.1
  246.3 6.6 %copy.34 = bf16[4,8,128,512]{3,2,1,0:T(8,128)(2,1)} copy(bf16[4,8,128,512]{3,1,0,2:T(8,128)(2,1)} %get-tuple-element.13) | data formatting | bytes 8388608
  252.9 0.2 convolution_subtract_fusion
  253.1 0.0 copy-done.1
  253.1 0.9 fusion.16
  (2 shorter events, 0.0 us)
Async XLA Ops:
  0.6 21.1 %copy-start = (bf16[1,1024,1024]{2,1,0:T(8,128)(2,1)S(1)}, bf16[1,1024,1024]{2,1,0:T(8,128)(2,1)}, u32[]{:S(2)}) copy-start(bf16[1,1024,1024]{2,1,0:T(8,128)(2,1)} %param.9) | copy-start | bytes 6291460
  9.0 100.5 %all-to-all-start.1 = ((bf16[4,1,1024,512]{3,0,1,2:T(4,128)(2,1)}), bf16[4,1,1024,512]{3,0,1,2:T(4,128)(2,1)}, u32[]{:S(2)}, u32[]{:S(2)}) async-start(bf16[4,1,1024,512]{3,0,1,2:T(4,128)(2,1)} %fusion.21), calls=%async_computation.1 | async-start | bytes 8388608 | tf_op jit(solution)/shard_map/all_to_all | solution.py:23
  36.0 78.3 %copy-start.5 = (s32[16]{0:T(128)S(1)}, s32[16]{0:T(128)}, u32[]{:S(2)}) copy-start(s32[16]{0:T(128)} %param.14) | copy-start | bytes 196
  36.0 78.4 %copy-start.2 = (bf16[128,8,8]{0,2,1:T(8,128)(2,1)S(1)}, bf16[128,8,8]{0,2,1:T(8,128)(2,1)}, u32[]{:S(2)}) copy-start(bf16[128,8,8]{0,2,1:T(8,128)(2,1)} %param.10) | copy-start | bytes 49156
  109.5 97.2 %all-to-all-start = ((bf16[4,1,1024,512]{3,0,1,2:T(4,128)(2,1)}), bf16[4,1,1024,512]{3,0,1,2:T(4,128)(2,1)}, u32[]{:S(2)}, u32[]{:S(2)}) async-start(bf16[4,1,1024,512]{3,0,1,2:T(4,128)(2,1)} %copy.28), calls=%async_computation | async-start | bytes 8388608 | tf_op jit(solution)/shard_map/all_to_all | solution.py:22
  117.7 89.0 %copy-start.3 = (f32[512]{0:T(512)S(1)}, f32[512]{0:T(512)}, u32[]{:S(2)}) copy-start(f32[512]{0:T(512)} %param.12) | copy-start | bytes 6148
  117.7 89.0 %copy-start.4 = (f32[512]{0:T(512)S(1)}, f32[512]{0:T(512)}, u32[]{:S(2)}) copy-start(f32[512]{0:T(512)} %param.11) | copy-start | bytes 6148
  246.3 6.8 %copy-start.1 = (f32[512,256]{1,0:T(8,128)S(1)}, f32[512,256]{1,0:T(8,128)}, u32[]{:S(2)}) copy-start(f32[512,256]{1,0:T(8,128)} %param.15) | copy-start | bytes 1572868
where the time goes:
time: 255 us; the launch traced here: 254 us
  waiting for transfers between devices  158 us (62%)
  blocking collectives  24.8 us (10%)
  matrix products  22.2 us (9%)
  other arithmetic  18.3 us (7%)
  local copies, waits for them, and re-layouts  17.8 us (7%)
  starting transfers between devices  12 us (5%)
    all_to_all x1, waiting for transfers between devices, shards(): lax.all_to_all(mixed, 'seq', split_axis=2, concat_axis=1, tiled=True)  84.6 us
    all_to_all x1, waiting for transfers between devices, shards(): lax.all_to_all(grid, 'seq', split_axis=2, concat_axis=1, tiled=True)  73.5 us
    psum x1, blocking collectives, shards(): mine = lax.psum(partial_value, 'seq') * scale_local[:, None]  19.6 us
    dot_general x1, matrix products, shards(): jnp.einsum('dpjc,jpq->dqjc', values_t, factor_two, preferred_element_type...  14.7 us
    mul x2, other arithmetic, shards(): tokens.reshape(doc_dev, blocks_dev, blk_size, chan)  12.9 us
    convert_element_type x1, local copies, waits for them, and re-layouts, shards(): mixed = jnp.einsum('dbic,bij->dbjc', grid, factor_one, preferred_element_...  7.88 us
    all_to_all x1, starting transfers between devices, shards(): lax.all_to_all(grid, 'seq', split_axis=2, concat_axis=1, tiled=True)  7.25 us
    unnamed x15, local copies, waits for them, and re-layouts  6.85 us
  transfers between devices with their start and end apart: 2, of which 2 were waited for; matrix products, arithmetic and copies ran while one was open for 11% of the time, Pallas kernels for 0%

commit v1 on v0

--- a/solution.py
+++ b/solution.py
@@ -19,7 +19,10 @@
         "dbic,bij->dbjc", grid, factor_one, preferred_element_type=jnp.float32
     ).astype(jnp.bfloat16)
     values_t, inputs_t = (
-        lax.all_to_all(mixed, "seq", split_axis=2, concat_axis=1, tiled=True),
+        jnp.concatenate(
+            lax.all_to_all(jnp.stack(jnp.split(mixed, lax.axis_size("seq"), axis=2)), "seq", 0, 0),
+            axis=1,
+        ),
         lax.all_to_all(grid, "seq", split_axis=2, concat_axis=1, tiled=True),
     )
     second = jnp.einsum("dpjc,jpq->dqjc", values_t, factor_two, preferred_element_type=jnp.float32)

time: 255 us -> 263 us (1.031)
  waiting for transfers between devices: 158 us -> 170 us
  matrix products: 22.2 us -> 13.3 us
  local copies, waits for them, and re-layouts: 17.8 us -> 26.4 us
  other arithmetic: 18.3 us -> 15.1 us
    all_to_all x1, waiting for transfers between devices: 73.5 us -> 84.2 us  [shards(): lax.all_to_all(grid, 'seq', split_axis=2, concat_axis=1, tiled=True)]
    reshape x0 -> x1, local copies, waits for them, and re-layouts: none -> 7.89 us  [shards(): jnp.concatenate(lax.all_to_all(jnp.stack(jnp.split(mixed, lax.axis_size('...]
    convert_element_type x1 -> x0, local copies, waits for them, and re-layouts: 7.88 us -> none  [shards(): mixed = jnp.einsum('dbic,bij->dbjc', grid, factor_one, preferred_element_...]
    dot_general x1, matrix products: 14.7 us -> 7.04 us  [shards(): jnp.einsum('dpjc,jpq->dqjc', values_t, factor_two, preferred_element_type...]
    unnamed x15 -> x24, local copies, waits for them, and re-layouts: 6.85 us -> 14.4 us
    convert_element_type x1, other arithmetic: 4.37 us -> 1.13 us  [shards(): gate = jax.nn.sigmoid(gate_gain * inputs_t.astype(jnp.float32) + gate_bias)]
  transfers between devices with their start and end apart: 2 -> 2, of which waited for: 2 -> 2; matrix products, arithmetic and copies ran while one was open for 11% -> 6% of each run, Pallas kernels for 0% -> 0%
where the time goes in v1:
time: 263 us; the launch traced here: 262 us
  waiting for transfers between devices  170 us (65%)
  local copies, waits for them, and re-layouts  26.4 us (10%)
  blocking collectives  24.8 us (9%)
  other arithmetic  15.1 us (6%)
  matrix products  13.3 us (5%)
  starting transfers between devices  12 us (5%)
    all_to_all x1, waiting for transfers between devices, shards(): lax.all_to_all(jnp.stack(jnp.split(mixed, lax.axis_size('seq'), axis=2)),...  85.8 us
    all_to_all x1, waiting for transfers between devices, shards(): lax.all_to_all(grid, 'seq', split_axis=2, concat_axis=1, tiled=True)  84.2 us
    psum x1, blocking collectives, shards(): mine = lax.psum(partial_value, 'seq') * scale_local[:, None]  19.6 us
    unnamed x24, local copies, waits for them, and re-layouts  14.4 us
    mul x2, other arithmetic, shards(): tokens.reshape(doc_dev, blocks_dev, blk_size, chan)  12.9 us
    reshape x1, local copies, waits for them, and re-layouts, shards(): jnp.concatenate(lax.all_to_all(jnp.stack(jnp.split(mixed, lax.axis_size('...  7.89 us
    all_to_all x1, starting transfers between devices, shards(): lax.all_to_all(jnp.stack(jnp.split(mixed, lax.axis_size('seq'), axis=2)),...  7.25 us
    dot_general x1, matrix products, shards(): jnp.einsum('dpjc,jpq->dqjc', values_t, factor_two, preferred_element_type...  7.04 us
  transfers between devices with their start and end apart: 2, of which 2 were waited for; matrix products, arithmetic and copies ran while one was open for 6% of the time, Pallas kernels for 0%

profile of v1, /device:TPU:0, one launch (start us, length us, event | category | flops | bytes accessed | tf_op | source)
XLA Modules:
  0.0 262.3 jit_solution(7599133529356304003)
XLA Ops:
  0.6 0.0 copy-start
  0.7 0.9 multiply_rsqrt_fusion
  1.5 5.4 %copy_multiply_fusion.1 = bf16[4,1024,512]{2,0,1:T(4,128)(2,1)S(1)} fusion(bf16[4,1024,512]{2,1,0:T(8,128)(2,1)} %param.8, bf16[4]{0:T(256)(128)(2,1)S(1)} %compare_convert_fusion), kind=kLoop, calls=%fused_computation.10 | loop fusion | flops 2097152 | bytes 8388616 | tf_op jit(solution)/shard_map/mul | solution.py:17
  7.0 0.0 copy-done
  7.0 5.2 %convert_bitcast_fusion = bf16[4,1,1024,512]{2,3,0,1:T(8,128)(2,1)S(1)} fusion(bf16[4,1024,512]{2,0,1:T(4,128)(2,1)S(1)} %copy_multiply_fusion.1, bf16[1,1024,1024]{2,1,0:T(8,128)(2,1)S(1)} %copy-done), kind=kOutput, calls=%fused_computation.11 | convolution fusion | flops 4297064448 | bytes 10485760 | tf_op jit(solution)/shard_map/dbic,bij->dbjc/dot_general | solution.py:18
  12.2 0.9 fusion.17
  13.1 0.9 fusion.16
  14.0 0.9 fusion.15
  15.0 0.9 fusion.14
  15.9 0.9 fusion.13
  16.9 0.9 fusion.12
  17.8 0.9 fusion.11
  18.7 1.0 fusion.10
  19.7 7.2 %all-to-all-start = ((bf16[8,4,1,128,512]{3,4,1,2,0:T(8,128)(2,1)}), bf16[8,4,1,128,512]{3,4,1,2,0:T(8,128)(2,1)}, u32[]{:S(2)}, u32[]{:S(2)}) async-start(bf16[8,4,1,128,512]{3,4,1,2,0:T(8,128)(2,1)} %fusion.10), calls=%async_computation | async-start | bytes 8388608 | tf_op jit(solution)/shard_map/all_to_all | solution.py:23
  26.9 7.5 %fusion.26 = bf16[4,1,1024,512]{3,0,1,2:T(4,128)(2,1)} fusion(bf16[4]{0:T(256)(128)(2,1)S(1)} %compare_convert_fusion, bf16[4,1024,512]{2,1,0:T(8,128)(2,1)} %param.8), kind=kLoop, calls=%fused_computation.38 | loop fusion | flops 2097152 | bytes 8388616 | tf_op jit(solution)/shard_map/mul | solution.py:17
  34.4 0.0 copy-start.6
  34.4 0.0 copy-start.3
  34.4 85.8 %all-to-all-done = bf16[8,4,1,128,512]{3,4,1,2,0:T(8,128)(2,1)} async-done(((bf16[8,4,1,128,512]{3,4,1,2,0:T(8,128)(2,1)}), bf16[8,4,1,128,512]{3,4,1,2,0:T(8,128)(2,1)}, u32[]{:S(2)}, u32[]{:S(2)}) %all-to-all-start) | async-done | bytes 4194336 | tf_op jit(solution)/shard_map/all_to_all | solution.py:23
  120.2 4.7 %all-to-all-start.1 = ((bf16[4,1,1024,512]{3,0,1,2:T(4,128)(2,1)}), bf16[4,1,1024,512]{3,0,1,2:T(4,128)(2,1)}, u32[]{:S(2)}, u32[]{:S(2)}) async-start(bf16[4,1,1024,512]{3,0,1,2:T(4,128)(2,1)} %fusion.26), calls=%async_computation.1 | async-start | bytes 8388608 | tf_op jit(solution)/shard_map/all_to_all | solution.py:26
  125.0 0.0 copy-done.6
  125.0 0.1 dynamic_slice.7
  125.0 0.0 copy-done.3
  125.0 0.2 copy.26
  125.2 0.1 fusion.18
  125.3 7.9 %copy.21 = bf16[4,8,128,512]{3,1,0,2:T(8,128)(2,1)} copy(bf16[4,8,128,512]{2,3,0,1:T(8,128)(2,1)} %bitcast.16) | data formatting | bytes 8388608 | tf_op jit(solution)/shard_map/reshape | solution.py:22
  133.2 84.2 %all-to-all-done.1 = bf16[4,1,1024,512]{3,0,1,2:T(4,128)(2,1)} async-done(((bf16[4,1,1024,512]{3,0,1,2:T(4,128)(2,1)}), bf16[4,1,1024,512]{3,0,1,2:T(4,128)(2,1)}, u32[]{:S(2)}, u32[]{:S(2)}) %all-to-all-start.1) | async-done | bytes 4194336 | tf_op jit(solution)/shard_map/all_to_all | solution.py:26
  217.4 3.0 %copy.23 = bf16[4,1,1024,512]{3,2,0,1:T(8,128)(2,1)S(1)} copy(bf16[4,1,1024,512]{3,0,1,2:T(4,128)(2,1)} %all-to-all-done.1) | data formatting | bytes 8388608 | tf_op jit(solution)/shard_map/all_to_all | solution.py:26
  220.4 0.0 copy-start.1
  220.4 0.0 copy-start.4
  220.5 0.0 copy-start.5
  220.5 1.1 convert.1
  221.6 1.0 copy-done.1
  222.6 0.0 copy-done.4
  222.6 0.0 copy-done.5
  222.6 7.0 %multiply_reduce_fusion = (f32[4,512]{1,0:T(4,128)S(1)}, bf16[4,8,128,512]{3,1,0,2:T(8,128)(2,1)}) fusion(f32[4,8]{1,0:T(4,128)S(1)} %fusion.18, f32[512]{0:T(512)S(1)} %copy-done.4, f32[4,8,128,512]{3,2,1,0:T(8,128)S(1)} %convert.1, f32[512]{0:T(512)S(1)} %copy-done.5, bf16[4,8,128,512]{3,1,0,2:T(8,128)(2,1)S(1)} %copy-done.1, ...), kind=kOutput, calls=%fused_computation.7 | convolution fusion | flops 52426752 | bytes 16806016 | tf_op jit(solution)/shard_map/dpjc,jpq->dqjc/dot_general | solution.py:28
  229.7 19.6 %psum.7 = f32[4,512]{1,0:T(4,128)S(1)} all-reduce(f32[4,512]{1,0:T(4,128)S(1)} %get-tuple-element.10), channel_id=1, replica_groups=mesh['seq'=8,'doc'=4] {'seq'}, use_global_device_ids=true, to_apply=%region_1.0 | all-reduce | flops 2048 | bytes 16384 | tf_op jit(solution)/shard_map/psum | solution.py:36
  249.3 0.1 multiply_bitcast_fusion
  249.4 5.2 %all-gather = f32[4,4,512]{2,1,0:T(4,128)S(1)} all-gather(f32[1,4,512]{2,1,0:T(4,128)S(1)} %multiply_bitcast_fusion), channel_id=1, replica_groups=mesh['seq'=8,'doc'=4] {'doc'}, dimensions={0}, use_global_device_ids=true | all-gather | bytes 40960 | tf_op jit(solution)/shard_map/all_gather | solution.py:37
  254.6 0.0 copy-start.2
  254.6 6.6 %copy.25 = bf16[4,8,128,512]{3,2,1,0:T(8,128)(2,1)} copy(bf16[4,8,128,512]{3,1,0,2:T(8,128)(2,1)} %get-tuple-element.11) | data formatting | bytes 8388608
  261.2 0.2 convolution_subtract_fusion
  261.4 0.0 copy-done.2
  261.4 0.9 fusion.20
  (2 shorter events, 0.0 us)
Async XLA Ops:
  0.6 6.4 %copy-start = (bf16[1,1024,1024]{2,1,0:T(8,128)(2,1)S(1)}, bf16[1,1024,1024]{2,1,0:T(8,128)(2,1)}, u32[]{:S(2)}) copy-start(bf16[1,1024,1024]{2,1,0:T(8,128)(2,1)} %param.9) | copy-start | bytes 6291460
  19.7 100.5 %all-to-all-start = ((bf16[8,4,1,128,512]{3,4,1,2,0:T(8,128)(2,1)}), bf16[8,4,1,128,512]{3,4,1,2,0:T(8,128)(2,1)}, u32[]{:S(2)}, u32[]{:S(2)}) async-start(bf16[8,4,1,128,512]{3,4,1,2,0:T(8,128)(2,1)} %fusion.10), calls=%async_computation | async-start | bytes 8388608 | tf_op jit(solution)/shard_map/all_to_all | solution.py:23
  34.4 90.6 %copy-start.6 = (s32[16]{0:T(128)S(1)}, s32[16]{0:T(128)}, u32[]{:S(2)}) copy-start(s32[16]{0:T(128)} %param.14) | copy-start | bytes 196
  34.4 90.7 %copy-start.3 = (bf16[128,8,8]{0,2,1:T(8,128)(2,1)S(1)}, bf16[128,8,8]{0,2,1:T(8,128)(2,1)}, u32[]{:S(2)}) copy-start(bf16[128,8,8]{0,2,1:T(8,128)(2,1)} %param.10) | copy-start | bytes 49156
  120.2 97.2 %all-to-all-start.1 = ((bf16[4,1,1024,512]{3,0,1,2:T(4,128)(2,1)}), bf16[4,1,1024,512]{3,0,1,2:T(4,128)(2,1)}, u32[]{:S(2)}, u32[]{:S(2)}) async-start(bf16[4,1,1024,512]{3,0,1,2:T(4,128)(2,1)} %fusion.26), calls=%async_computation.1 | async-start | bytes 8388608 | tf_op jit(solution)/shard_map/all_to_all | solution.py:26
  220.4 2.2 copy-start.1
  220.4 2.2 copy-start.4
  220.5 2.2 copy-start.5
  254.6 6.8 %copy-start.2 = (f32[512,256]{1,0:T(8,128)S(1)}, f32[512,256]{1,0:T(8,128)}, u32[]{:S(2)}) copy-start(f32[512,256]{1,0:T(8,128)} %param.15) | copy-start | bytes 1572868
